TPU v7x, 32 devices: a whole 2x2x4 slice. The times are simulated.
32 devices in a mesh: dp: 8 (over z, core), ctx: 4 (over y, x).
Axes of the slice: x: 2, y: 2, z: 4, core: 2. Of those that a mesh axis runs over, the one named last changes fastest.
Arguments:
- queries: bfloat16 [8, 512, 1024], P('dp', 'ctx'), may hold values from -6 to 6
- key_vectors: bfloat16 [8, 512, 1024], P('dp', 'ctx'), may hold values from -6 to 6
- values: bfloat16 [8, 512, 1024], P('dp', 'ctx'), may hold values from -6 to 6
- cotangent: bfloat16 [8, 512, 1024], P('dp', 'ctx'), may hold values from -6 to 6
- lengths: int32 [8], P('dp'), may hold values from 128 to 512
- conv_taps: float32 [31, 1024], replicated, may hold values from -3 to 3
Outputs:
- conv_out: bfloat16 [8, 512, 1024], P('dp', 'ctx')
- query_grad: bfloat16 [8, 512, 1024], P('dp', 'ctx')
- key_grad: bfloat16 [8, 512, 1024], P('dp', 'ctx')
- value_grad: bfloat16 [8, 512, 1024], P('dp', 'ctx')
- taps_grad: float32 [31, 1024], replicated
All inputs are finite; a program needn't handle non-finite values.
Results may differ from a plain program's by a relative error of at most 0.024.
Values may be sent and summed in bfloat16 or wider, within the bound.
No kernel may reach another device: no remote copies, remote signals or barrier semaphores. Data moves between devices by JAX's collectives and lax.ppermute only.
A program may use at most 64 MiB of HBM per device.

v0:
```python
import jax
import jax.numpy as jnp
from jax import lax
from jax.sharding import PartitionSpec as P

HEAD_DIM = 64
KERNEL = 31


def with_halo(block, sides, width):
    for axis, dim in sides:
        count = lax.axis_size(axis)
        forward = [(i, i + 1) for i in range(count - 1)]
        backward = [(target, source) for source, target in forward]
        low = lax.ppermute(
            lax.slice_in_dim(block, block.shape[dim] - width, None, axis=dim), axis, forward
        )
        high = lax.ppermute(lax.slice_in_dim(block, 0, width, axis=dim), axis, backward)
        block = jnp.concatenate([low, block, high], axis=dim)
    return block


def attend_forward(query_heads, key_heads, value_heads, valid_keys, block_rows):
    block_count = query_heads.shape[0] // block_rows
    score_scale = HEAD_DIM ** (-0.5)

    def one_block(offset):
        query_part = lax.dynamic_slice_in_dim(query_heads, offset, block_rows, 0)
        scores = (
            jnp.einsum("qhd,khd->hqk", query_part, key_heads, preferred_element_type=jnp.float32)
            * score_scale
        )
        scores = jnp.where(valid_keys[None, None, :], scores, -1e30)
        row_top = jnp.max(scores, axis=2, keepdims=True)
        log_total = row_top + jnp.log(jnp.sum(jnp.exp(scores - row_top), axis=2, keepdims=True))
        softmax_bf = jnp.exp(scores - log_total).astype(jnp.bfloat16)
        attended = jnp.einsum(
            "hqk,khd->qhd", softmax_bf, value_heads, preferred_element_type=jnp.float32
        ).astype(jnp.bfloat16)
        return (attended, log_total[:, :, 0])

    offsets = jnp.arange(block_count, dtype=jnp.int32) * block_rows
    attended, log_totals = lax.map(one_block, offsets)
    return (attended.reshape(query_heads.shape), log_totals)


def attend_backward(
    query_heads, key_heads, value_heads, out_heads, grad_heads, log_totals, valid_keys, block_rows
):
    block_count = query_heads.shape[0] // block_rows
    score_scale = HEAD_DIM ** (-0.5)

    def one_block(carried, inputs):
        offset, log_part = inputs
        key_acc, value_acc = carried
        query_part = lax.dynamic_slice_in_dim(query_heads, offset, block_rows, 0)
        out_part = lax.dynamic_slice_in_dim(out_heads, offset, block_rows, 0)
        grad_part = lax.dynamic_slice_in_dim(grad_heads, offset, block_rows, 0)
        scores = (
            jnp.einsum("qhd,khd->hqk", query_part, key_heads, preferred_element_type=jnp.float32)
            * score_scale
        )
        scores = jnp.where(valid_keys[None, None, :], scores, -1e30)
        softmax = jnp.exp(scores - log_part[:, :, None])
        row_delta = jnp.sum(grad_part.astype(jnp.float32) * out_part.astype(jnp.float32), axis=2).T
        prob_grad = jnp.einsum(
            "qhd,khd->hqk", grad_part, value_heads, preferred_element_type=jnp.float32
        )
        score_grad = (softmax * (prob_grad - row_delta[:, :, None])).astype(jnp.bfloat16)
        query_grad = (
            jnp.einsum("hqk,khd->qhd", score_grad, key_heads, preferred_element_type=jnp.float32)
            * score_scale
        ).astype(jnp.bfloat16)
        key_acc = key_acc + jnp.einsum(
            "hqk,qhd->khd", score_grad, query_part, preferred_element_type=jnp.float32
        )
        value_acc = value_acc + jnp.einsum(
            "hqk,qhd->khd",
            softmax.astype(jnp.bfloat16),
            grad_part,
            preferred_element_type=jnp.float32,
        )
        return ((key_acc, value_acc), query_grad)

    offsets = jnp.arange(block_count, dtype=jnp.int32) * block_rows
    zeros_acc = jnp.zeros(key_heads.shape, jnp.float32)
    (key_acc, value_acc), query_grad = lax.scan(
        one_block, (zeros_acc, zeros_acc), (offsets, log_totals)
    )
    key_grad = (key_acc * score_scale).astype(jnp.bfloat16)
    return (query_grad.reshape(query_heads.shape), key_grad, value_acc.astype(jnp.bfloat16))


def conv_terms(padded_in, padded_cot, conv_taps, rows):
    half_width = KERNEL // 2
    conv_sum = jnp.zeros((rows, conv_taps.shape[1]), jnp.float32)
    back_sum = jnp.zeros((rows, conv_taps.shape[1]), jnp.float32)
    cot_rows = padded_cot[half_width : half_width + rows].astype(jnp.float32)
    tap_rows = []
    for tap_index in range(KERNEL):
        window = padded_in[tap_index : tap_index + rows]
        conv_sum = conv_sum + conv_taps[tap_index] * window
        back_sum = (
            back_sum
            + conv_taps[tap_index]
            * padded_cot[2 * half_width - tap_index : 2 * half_width - tap_index + rows]
        )
        tap_rows.append(jnp.sum(cot_rows * window, axis=0))
    return (conv_sum, back_sum, jnp.stack(tap_rows))


def split_heads(flat_rows):
    return flat_rows.reshape(flat_rows.shape[0], flat_rows.shape[1] // HEAD_DIM, HEAD_DIM)


def per_device(queries, key_vectors, values, cotangent, lengths, conv_taps):
    tok_rows = queries.shape[1]
    width = queries.shape[2]
    ctx_count = lax.axis_size("ctx")
    frames = tok_rows * ctx_count
    local_width = width // ctx_count
    block_rows = min(512, frames)
    half_width = KERNEL // 2
    length = lengths[0]
    valid_keys = jnp.arange(frames, dtype=jnp.int32) < length
    stacked = jnp.stack([queries[0], key_vectors[0], values[0]])
    exchanged = lax.all_to_all(stacked, "ctx", split_axis=2, concat_axis=1, tiled=True)
    query_heads = split_heads(exchanged[0])
    key_heads = split_heads(exchanged[1])
    value_heads = split_heads(exchanged[2])
    out_heads, log_totals = attend_forward(
        query_heads, key_heads, value_heads, valid_keys, block_rows
    )
    out_frames = lax.all_to_all(
        out_heads.reshape(frames, local_width), "ctx", split_axis=0, concat_axis=1, tiled=True
    )
    positions = lax.axis_index("ctx") * tok_rows + jnp.arange(tok_rows, dtype=jnp.int32)
    valid_rows = positions < length
    kept = jnp.where(valid_rows[:, None], out_frames, jnp.zeros_like(out_frames))
    padded_cot = with_halo(cotangent[0], (("ctx", 0),), half_width)
    padded_in = with_halo(kept, (("ctx", 0),), half_width)
    conv_sum, back_sum, taps_part = conv_terms(padded_in, padded_cot, conv_taps, tok_rows)
    conv_out = conv_sum.astype(jnp.bfloat16)
    taps_grad = lax.psum(taps_part, ("dp", "ctx"))
    grad_rows = jnp.where(valid_rows[:, None], back_sum, jnp.zeros_like(back_sum)).astype(
        jnp.bfloat16
    )
    grad_heads = split_heads(
        lax.all_to_all(grad_rows, "ctx", split_axis=1, concat_axis=0, tiled=True)
    )
    query_grad, key_grad, value_grad = attend_backward(
        query_heads,
        key_heads,
        value_heads,
        out_heads,
        grad_heads,
        log_totals,
        valid_keys,
        block_rows,
    )
    grads_stacked = jnp.stack(
        [
            query_grad.reshape(frames, local_width),
            key_grad.reshape(frames, local_width),
            value_grad.reshape(frames, local_width),
        ]
    )
    grads_rows = lax.all_to_all(grads_stacked, "ctx", split_axis=1, concat_axis=2, tiled=True)
    return (
        conv_out[None],
        grads_rows[0][None],
        grads_rows[1][None],
        grads_rows[2][None],
        taps_grad,
    )


def solution(mesh):
    return jax.shard_map(
        per_device,
        mesh=mesh,
        in_specs=(
            P("dp", "ctx", None),
            P("dp", "ctx", None),
            P("dp", "ctx", None),
            P("dp", "ctx", None),
            P("dp"),
            P(),
        ),
        out_specs=(
            P("dp", "ctx", None),
            P("dp", "ctx", None),
            P("dp", "ctx", None),
            P("dp", "ctx", None),
            P(),
        ),
        check_vma=False,
    )
```

profile of v0, /device:TPU:0, one launch (start us, length us, event | category | flops | bytes accessed | tf_op | source)
XLA Modules:
  0.0 237.2 jit_solution(9200691849444188628)
XLA Ops:
  7.2 0.8 slice_bitcast_fusion.1
  8.0 1.3 collective-permute-start.2
  9.3 5.5 %collective-permute-start.3 = (bf16[15,1024]{1,0:T(8,128)(2,1)S(1)}, bf16[15,1024]{1,0:T(8,128)(2,1)S(1)}, u32[]{:S(2)}, u32[]{:S(2)}) collective-permute-start(bf16[15,1024]{1,0:T(8,128)(2,1)S(1)} %get-tuple-element.97), channel_id=1, source_target_pairs={{0,1},{1,2},{2,3},{4,5},{5,6},{6,7},{8,9},{9,10},{10,11},{12,13},{... | collective-permute-start | bytes 92168 | tf_op jit(solution)/shard_map/ppermute | solution.py:15
  14.8 1.1 fusion.144
  15.9 1.4 fusion.143
  17.9 0.0 collective-permute-done.2
  17.9 0.0 collective-permute-done.3
  17.9 8.8 %select_convert_fusion = bf16[128,1024]{1,0:T(8,128)(2,1)S(1)} fusion(bf16[128,1024]{1,0:T(8,128)(2,1)} %bitcast.149, bf16[15,1024]{1,0:T(8,128)(2,1)S(1)} %collective-permute-done.3, bf16[15,1024]{1,0:T(8,128)(2,1)S(1)} %collective-permute-done.2, f32[1024]{0:T(1024)S(1)} %bitcast.177, f32[1024]{0:T(1024)S(1)} %bitcast.179, f32[1024]{0:T(1024)S(1)} %bitcast.183, ...), kind=kLoop, calls=%fused_computation.214 | loop fusion | flops 24117248 | bytes 712832 | tf_op jit(solution)/shard_map/convert_element_type | solution.py:145
  26.8 0.8 copy.44
  27.6 4.3 %all-to-all-start.2 = ((bf16[128,4,256]{0,2,1:T(8,128)(2,1)}), bf16[128,4,256]{0,2,1:T(8,128)(2,1)S(1)}, u32[]{:S(2)}, u32[]{:S(2)}) async-start(bf16[128,4,256]{0,2,1:T(8,128)(2,1)} %bitcast.41), calls=%async_computation.2 | async-start | bytes 524288 | tf_op jit(solution)/shard_map/all_to_all | solution.py:149
  31.9 1.2 pad_maximum_fusion.1
  33.1 1.4 copy.39
  34.5 2.7 %all-to-all-done.2 = bf16[128,4,256]{0,2,1:T(8,128)(2,1)S(1)} async-done(((bf16[128,4,256]{0,2,1:T(8,128)(2,1)}), bf16[128,4,256]{0,2,1:T(8,128)(2,1)S(1)}, u32[]{:S(2)}, u32[]{:S(2)}) %all-to-all-start.2) | async-done | bytes 262176 | tf_op jit(solution)/shard_map/all_to_all | solution.py:149
  37.3 3.5 %all-to-all-start = ((bf16[3,128,1024]{1,0,2:T(4,128)(2,1)}), bf16[3,128,1024]{1,0,2:T(4,128)(2,1)S(1)}, u32[]{:S(2)}, u32[]{:S(2)}) async-start(bf16[3,128,1024]{1,0,2:T(4,128)(2,1)} %copy.39), calls=%async_computation | async-start | bytes 2097152 | tf_op jit(solution)/shard_map/all_to_all | solution.py:127
  40.8 0.2 copy.45
  41.0 0.1 reshape.60
  41.1 11.9 %all-to-all-done = bf16[3,128,1024]{1,0,2:T(4,128)(2,1)S(1)} async-done(((bf16[3,128,1024]{1,0,2:T(4,128)(2,1)}), bf16[3,128,1024]{1,0,2:T(4,128)(2,1)S(1)}, u32[]{:S(2)}, u32[]{:S(2)}) %all-to-all-start) | async-done | bytes 786464 | tf_op jit(solution)/shard_map/all_to_all | solution.py:127
  53.0 0.7 copy.62
  53.8 0.3 fusion.141
  54.1 0.1 reshape_squeeze.11
  54.2 0.1 reshape_squeeze.10
  54.3 0.1 reshape_squeeze.9
  54.4 1.0 fusion.1
  55.4 0.9 exponential_reduce_fusion
  56.3 0.8 fusion
  57.2 0.7 convolution_convert_fusion
  57.9 1.2 multiply_reduce_fusion
  59.1 1.5 multiply_convert_fusion
  60.6 1.5 fusion.3
  62.1 0.4 copy.52
  62.5 2.0 copy.51
  64.5 1.0 all_to_all.51
  65.5 0.7 copy.42
  66.2 4.0 %all-to-all-start.1 = ((bf16[4,128,256]{1,2,0:T(8,128)(2,1)}), bf16[4,128,256]{1,2,0:T(8,128)(2,1)}, u32[]{:S(2)}, u32[]{:S(2)}) async-start(bf16[4,128,256]{1,2,0:T(8,128)(2,1)} %copy.42), calls=%async_computation.1 | async-start | bytes 524288 | tf_op jit(solution)/shard_map/all_to_all | solution.py:134
  70.3 0.0 copy-start
  70.3 0.5 fusion.2
  70.7 0.4 copy.50
  71.2 4.5 %all-to-all-done.1 = bf16[4,128,256]{1,2,0:T(8,128)(2,1)} async-done(((bf16[4,128,256]{1,2,0:T(8,128)(2,1)}), bf16[4,128,256]{1,2,0:T(8,128)(2,1)}, u32[]{:S(2)}, u32[]{:S(2)}) %all-to-all-start.1) | async-done | bytes 262176 | tf_op jit(solution)/shard_map/all_to_all | solution.py:134
  75.7 1.1 copy.43
  76.8 0.1 broadcast_select_fusion
  76.9 3.4 %collective-permute-start = (bf16[15,1024]{1,0:T(8,128)(2,1)S(1)}, bf16[15,1024]{1,0:T(8,128)(2,1)S(1)}, u32[]{:S(2)}, u32[]{:S(2)}) collective-permute-start(bf16[15,1024]{1,0:T(8,128)(2,1)S(1)} %get-tuple-element.98), channel_id=1, source_target_pairs={{0,1},{1,2},{2,3},{4,5},{5,6},{6,7},{8,9},{9,10},{10,11},{12,13},{... | collective-permute-start | bytes 92168 | tf_op jit(solution)/shard_map/ppermute | solution.py:15
  80.3 3.8 %pad_maximum_fusion = bf16[3,512,256]{2,0,1:T(4,128)(2,1)} fusion(bf16[1,512,256]{2,0,1:T(2,128)(2,1)S(1)} %copy.52, bf16[1,512,256]{2,0,1:T(2,128)(2,1)} %copy.51, bf16[1,512,256]{2,0,1:T(2,128)(2,1)S(1)} %copy.50), kind=kLoop, calls=%fused_computation.101 | loop fusion | flops 2359296 | bytes 1572864 | tf_op jit(solution)/shard_map/stack | solution.py:161
  84.1 3.5 %all-to-all-start.3 = ((bf16[3,512,256]{2,0,1:T(4,128)(2,1)}), bf16[3,512,256]{2,0,1:T(4,128)(2,1)S(1)}, u32[]{:S(2)}, u32[]{:S(2)}) async-start(bf16[3,512,256]{2,0,1:T(4,128)(2,1)} %pad_maximum_fusion), calls=%async_computation.3 | async-start | bytes 2097152 | tf_op jit(solution)/shard_map/all_to_all | solution.py:168
  87.6 0.0 all-reduce.2.cloned.1.call-start
  87.7 1.3 collective-permute-start.1
  89.0 0.0 collective-permute-done
  89.0 0.7 fusion.66
  89.7 0.5 fusion.65
  90.2 9.8 %collective-permute-done.1 = bf16[15,1024]{1,0:T(8,128)(2,1)S(1)} collective-permute-done((bf16[15,1024]{1,0:T(8,128)(2,1)S(1)}, bf16[15,1024]{1,0:T(8,128)(2,1)S(1)}, u32[]{:S(2)}, u32[]{:S(2)}) %collective-permute-start.1) | collective-permute-done | bytes 30752 | tf_op jit(solution)/shard_map/ppermute | solution.py:18
  100.0 0.5 fusion.81
  100.6 0.7 fusion.82
  101.2 2.7 %stack.135 = f32[31,1024]{1,0:T(8,128)} concatenate(f32[1,1024]{1,0:T(1,128)S(1)} %bitcast.220, f32[1,1024]{1,0:T(1,128)S(1)} %bitcast.221, f32[1,1024]{1,0:T(1,128)S(1)} %bitcast.222, f32[1,1024]{1,0:T(1,128)S(1)} %bitcast.223, f32[1,1024]{1,0:T(1,128)S(1)} %bitcast.224, f32[1,1024]{1,0:T(1,128)S(1)} %bitcast.225, f32[1,1024]{1,0:T(1,128)S(1)} %bitcast.226, ...), dimensions={0} | concatenate | bytes 253952 | tf_op jit(solution)/shard_map/stack | solution.py:109
  103.9 0.0 all-reduce.2.cloned.1.call-update
  103.9 3.1 %fusion.139 = bf16[1,128,1024]{2,1,0:T(8,128)(2,1)} fusion(bf16[15,1024]{1,0:T(8,128)(2,1)S(1)} %collective-permute-done.1, bf16[128,1024]{1,0:T(8,128)(2,1)S(1)} %broadcast_select_fusion, f32[1024]{0:T(1024)S(1)} %bitcast.178, f32[1024]{0:T(1024)S(1)} %bitcast.180, f32[1024]{0:T(1024)S(1)} %bitcast.184, f32[1024]{0:T(1024)S(1)} %bitcast.186, ...), kind=kLoop, calls=%fused_computation.296 | loop fusion | flops 23986176 | bytes 712704 | tf_op jit(solution)/shard_map/broadcast_in_dim | solution.py:170
  107.1 0.0 all-to-all-done.3
  107.1 1.1 fusion.140
  108.2 0.3 copy.55
  108.5 0.9 slice.517
  109.4 0.3 copy.54
  109.7 0.9 slice.515
  110.6 0.3 copy.53
  111.0 0.9 slice.513
  111.8 117.0 %all-reduce.2.cloned.1.call-done = f32[31,1024]{1,0:T(8,128)} async-done(((f32[31,1024]{1,0:T(8,128)}), f32[31,1024]{1,0:T(8,128)}) %all-reduce.2.cloned.1.call-update) | async-done | bytes 126992 | tf_op jit(solution)/shard_map/psum | solution.py:144
  228.8 1.6 copy.65
  (5 shorter events, 0.0 us)
Async XLA Ops:
  8.0 10.0 %collective-permute-start.2 = (bf16[15,1024]{1,0:T(8,128)(2,1)S(1)}, bf16[15,1024]{1,0:T(8,128)(2,1)S(1)}, u32[]{:S(2)}, u32[]{:S(2)}) collective-permute-start(bf16[15,1024]{1,0:T(8,128)(2,1)S(1)} %get-tuple-element.96), channel_id=1, source_target_pairs={{1,0},{2,1},{3,2},{5,4},{6,5},{7,6},{9,8},{10,9},{11,10},{13,12},{... | collective-permute-start | bytes 92168 | tf_op jit(solution)/shard_map/ppermute | solution.py:18
  9.3 8.7 %collective-permute-start.3 = (bf16[15,1024]{1,0:T(8,128)(2,1)S(1)}, bf16[15,1024]{1,0:T(8,128)(2,1)S(1)}, u32[]{:S(2)}, u32[]{:S(2)}) collective-permute-start(bf16[15,1024]{1,0:T(8,128)(2,1)S(1)} %get-tuple-element.97), channel_id=1, source_target_pairs={{0,1},{1,2},{2,3},{4,5},{5,6},{6,7},{8,9},{9,10},{10,11},{12,13},{... | collective-permute-start | bytes 92168 | tf_op jit(solution)/shard_map/ppermute | solution.py:15
  27.6 9.7 %all-to-all-start.2 = ((bf16[128,4,256]{0,2,1:T(8,128)(2,1)}), bf16[128,4,256]{0,2,1:T(8,128)(2,1)S(1)}, u32[]{:S(2)}, u32[]{:S(2)}) async-start(bf16[128,4,256]{0,2,1:T(8,128)(2,1)} %bitcast.41), calls=%async_computation.2 | async-start | bytes 524288 | tf_op jit(solution)/shard_map/all_to_all | solution.py:149
  37.3 15.8 %all-to-all-start = ((bf16[3,128,1024]{1,0,2:T(4,128)(2,1)}), bf16[3,128,1024]{1,0,2:T(4,128)(2,1)S(1)}, u32[]{:S(2)}, u32[]{:S(2)}) async-start(bf16[3,128,1024]{1,0,2:T(4,128)(2,1)} %copy.39), calls=%async_computation | async-start | bytes 2097152 | tf_op jit(solution)/shard_map/all_to_all | solution.py:127
  66.2 9.5 %all-to-all-start.1 = ((bf16[4,128,256]{1,2,0:T(8,128)(2,1)}), bf16[4,128,256]{1,2,0:T(8,128)(2,1)}, u32[]{:S(2)}, u32[]{:S(2)}) async-start(bf16[4,128,256]{1,2,0:T(8,128)(2,1)} %copy.42), calls=%async_computation.1 | async-start | bytes 524288 | tf_op jit(solution)/shard_map/all_to_all | solution.py:134
  70.3 18.7 %copy-start = (bf16[1,128,1024]{2,1,0:T(8,128)(2,1)S(1)}, bf16[1,128,1024]{2,1,0:T(8,128)(2,1)}, u32[]{:S(2)}) copy-start(bf16[1,128,1024]{2,1,0:T(8,128)(2,1)} %param.9) | copy-start | bytes 786436
  76.9 12.1 %collective-permute-start = (bf16[15,1024]{1,0:T(8,128)(2,1)S(1)}, bf16[15,1024]{1,0:T(8,128)(2,1)S(1)}, u32[]{:S(2)}, u32[]{:S(2)}) collective-permute-start(bf16[15,1024]{1,0:T(8,128)(2,1)S(1)} %get-tuple-element.98), channel_id=1, source_target_pairs={{0,1},{1,2},{2,3},{4,5},{5,6},{6,7},{8,9},{9,10},{10,11},{12,13},{... | collective-permute-start | bytes 92168 | tf_op jit(solution)/shard_map/ppermute | solution.py:15
  84.1 23.0 %all-to-all-start.3 = ((bf16[3,512,256]{2,0,1:T(4,128)(2,1)}), bf16[3,512,256]{2,0,1:T(4,128)(2,1)S(1)}, u32[]{:S(2)}, u32[]{:S(2)}) async-start(bf16[3,512,256]{2,0,1:T(4,128)(2,1)} %pad_maximum_fusion), calls=%async_computation.3 | async-start | bytes 2097152 | tf_op jit(solution)/shard_map/all_to_all | solution.py:168
  87.6 141.2 %all-reduce.2.cloned.1.call-start = ((), (), s32[]{:S(2)}) async-start(), calls=%async_computation.4 | async-start | bytes 262144 | tf_op jit(solution)/shard_map/psum | solution.py:144
  87.7 12.3 %collective-permute-start.1 = (bf16[15,1024]{1,0:T(8,128)(2,1)S(1)}, bf16[15,1024]{1,0:T(8,128)(2,1)S(1)}, u32[]{:S(2)}, u32[]{:S(2)}) collective-permute-start(bf16[15,1024]{1,0:T(8,128)(2,1)S(1)} %get-tuple-element.99), channel_id=1, source_target_pairs={{1,0},{2,1},{3,2},{5,4},{6,5},{7,6},{9,8},{10,9},{11,10},{13,12},{... | collective-permute-start | bytes 92168 | tf_op jit(solution)/shard_map/ppermute | solution.py:18
Sparse Core Ops, SparseCore 0:
  104.0 124.7 all-reduce.1
where the time goes:
time: 238 us; the launch traced here: 237 us
  waiting for transfers between devices  146 us (61%)
  starting transfers between devices  26.8 us (11%)
  local copies, waits for them, and re-layouts  21.8 us (9%)
  other arithmetic  21.2 us (9%)
  between operations  15 us (6%)
  matrix products  6.35 us (3%)
    psum x1, waiting for transfers between devices, per_device(): taps_grad = lax.psum(taps_part, ('dp', 'ctx'))  117 us
    all_to_all x1, waiting for transfers between devices, per_device(): lax.all_to_all(stacked, 'ctx', split_axis=2, concat_axis=1, tiled=True)  11.9 us
    ppermute x2, waiting for transfers between devices, with_halo(): lax.ppermute(lax.slice_in_dim(block, 0, width, axis=dim), axis, backward)  9.84 us
    ppermute x2, starting transfers between devices, with_halo(): lax.ppermute(lax.slice_in_dim(block, block.shape[dim] - width, None, axis...  8.85 us
    convert_element_type x1, other arithmetic, per_device(): jnp.where(valid_rows[:, None], back_sum, jnp.zeros_like(back_sum))  8.83 us
  transfers between devices with their start and end apart: 9, of which 5 were waited for; matrix products, arithmetic and copies ran while one was open for 10% of the time, Pallas kernels for 0%

commit v1 on v0

--- a/solution.py
+++ b/solution.py
@@ -141,7 +141,9 @@
     padded_in = with_halo(kept, (("ctx", 0),), half_width)
     conv_sum, back_sum, taps_part = conv_terms(padded_in, padded_cot, conv_taps, tok_rows)
     conv_out = conv_sum.astype(jnp.bfloat16)
-    taps_grad = lax.psum(taps_part, ("dp", "ctx"))
+    taps_grad = taps_part
+    for name in ("ctx", "dp"):
+        taps_grad = lax.psum(taps_grad, name)
     grad_rows = jnp.where(valid_rows[:, None], back_sum, jnp.zeros_like(back_sum)).astype(
         jnp.bfloat16
     )

time: 238 us -> 213 us (0.89)
  waiting for transfers between devices: 146 us -> 121 us
    psum x1 -> x2, waiting for transfers between devices: 117 us -> 91.9 us  [per_device(): taps_grad = lax.psum(taps_grad, name)]
  transfers between devices with their start and end apart: 9 -> 10, of which waited for: 5 -> 6; matrix products, arithmetic and copies ran while one was open for 10% -> 11% of each run, Pallas kernels for 0% -> 0%
where the time goes in v1:
time: 213 us; the launch traced here: 212 us
  waiting for transfers between devices  121 us (57%)
  starting transfers between devices  26.9 us (13%)
  local copies, waits for them, and re-layouts  21.8 us (10%)
  other arithmetic  21.2 us (10%)
  between operations  15 us (7%)
  matrix products  6.35 us (3%)
    psum x2, waiting for transfers between devices, per_device(): taps_grad = lax.psum(taps_grad, name)  91.9 us
    all_to_all x1, waiting for transfers between devices, per_device(): lax.all_to_all(stacked, 'ctx', split_axis=2, concat_axis=1, tiled=True)  11.9 us
    ppermute x2, waiting for transfers between devices, with_halo(): lax.ppermute(lax.slice_in_dim(block, 0, width, axis=dim), axis, backward)  9.84 us
    ppermute x2, starting transfers between devices, with_halo(): lax.ppermute(lax.slice_in_dim(block, block.shape[dim] - width, None, axis...  8.85 us
    convert_element_type x1, other arithmetic, per_device(): jnp.where(valid_rows[:, None], back_sum, jnp.zeros_like(back_sum))  8.83 us
    all_to_all x1, waiting for transfers between devices, per_device(): lax.all_to_all(out_heads.reshape(frames, local_width), 'ctx', split_axis=...  4.51 us
    all_to_all x1, starting transfers between devices, per_device(): lax.all_to_all(grad_rows, 'ctx', split_axis=1, concat_axis=0, tiled=True)  4.29 us
  transfers between devices with their start and end apart: 10, of which 6 were waited for; matrix products, arithmetic and copies ran while one was open for 11% of the time, Pallas kernels for 0%

profile of v1, /device:TPU:0, one launch (start us, length us, event | category | flops | bytes accessed | tf_op | source)
XLA Modules:
  0.0 212.2 jit_solution(1254793234149452821)
XLA Ops:
  7.2 0.8 slice_bitcast_fusion.1
  8.0 1.3 collective-permute-start.2
  9.3 5.5 %collective-permute-start.3 = (bf16[15,1024]{1,0:T(8,128)(2,1)S(1)}, bf16[15,1024]{1,0:T(8,128)(2,1)S(1)}, u32[]{:S(2)}, u32[]{:S(2)}) collective-permute-start(bf16[15,1024]{1,0:T(8,128)(2,1)S(1)} %get-tuple-element.97), channel_id=1, source_target_pairs={{0,1},{1,2},{2,3},{4,5},{5,6},{6,7},{8,9},{9,10},{10,11},{12,13},{... | collective-permute-start | bytes 92168 | tf_op jit(solution)/shard_map/ppermute | solution.py:15
  14.8 1.1 fusion.144
  15.9 1.4 fusion.143
  17.9 0.0 collective-permute-done.2
  17.9 8.8 %select_convert_fusion = bf16[128,1024]{1,0:T(8,128)(2,1)S(1)} fusion(bf16[128,1024]{1,0:T(8,128)(2,1)} %bitcast.149, bf16[15,1024]{1,0:T(8,128)(2,1)S(1)} %collective-permute-done.3, bf16[15,1024]{1,0:T(8,128)(2,1)S(1)} %collective-permute-done.2, f32[1024]{0:T(1024)S(1)} %bitcast.177, f32[1024]{0:T(1024)S(1)} %bitcast.179, f32[1024]{0:T(1024)S(1)} %bitcast.183, ...), kind=kLoop, calls=%fused_computation.214 | loop fusion | flops 24117248 | bytes 712832 | tf_op jit(solution)/shard_map/convert_element_type | solution.py:147
  26.8 0.8 copy.44
  27.6 4.3 %all-to-all-start.2 = ((bf16[128,4,256]{0,2,1:T(8,128)(2,1)}), bf16[128,4,256]{0,2,1:T(8,128)(2,1)S(1)}, u32[]{:S(2)}, u32[]{:S(2)}) async-start(bf16[128,4,256]{0,2,1:T(8,128)(2,1)} %bitcast.41), calls=%async_computation.2 | async-start | bytes 524288 | tf_op jit(solution)/shard_map/all_to_all | solution.py:151
  31.9 1.2 pad_maximum_fusion.1
  33.1 1.4 copy.39
  34.5 2.7 %all-to-all-done.2 = bf16[128,4,256]{0,2,1:T(8,128)(2,1)S(1)} async-done(((bf16[128,4,256]{0,2,1:T(8,128)(2,1)}), bf16[128,4,256]{0,2,1:T(8,128)(2,1)S(1)}, u32[]{:S(2)}, u32[]{:S(2)}) %all-to-all-start.2) | async-done | bytes 262176 | tf_op jit(solution)/shard_map/all_to_all | solution.py:151
  37.3 3.5 %all-to-all-start = ((bf16[3,128,1024]{1,0,2:T(4,128)(2,1)}), bf16[3,128,1024]{1,0,2:T(4,128)(2,1)S(1)}, u32[]{:S(2)}, u32[]{:S(2)}) async-start(bf16[3,128,1024]{1,0,2:T(4,128)(2,1)} %copy.39), calls=%async_computation | async-start | bytes 2097152 | tf_op jit(solution)/shard_map/all_to_all | solution.py:127
  40.8 0.2 copy.45
  41.0 0.1 reshape.60
  41.1 11.9 %all-to-all-done = bf16[3,128,1024]{1,0,2:T(4,128)(2,1)S(1)} async-done(((bf16[3,128,1024]{1,0,2:T(4,128)(2,1)}), bf16[3,128,1024]{1,0,2:T(4,128)(2,1)S(1)}, u32[]{:S(2)}, u32[]{:S(2)}) %all-to-all-start) | async-done | bytes 786464 | tf_op jit(solution)/shard_map/all_to_all | solution.py:127
  53.0 0.7 copy.62
  53.8 0.3 fusion.141
  54.1 0.1 reshape_squeeze.11
  54.2 0.1 reshape_squeeze.10
  54.3 0.1 reshape_squeeze.9
  54.4 1.0 fusion.1
  55.4 0.9 exponential_reduce_fusion
  56.3 0.8 fusion
  57.2 0.7 convolution_convert_fusion
  57.9 1.2 multiply_reduce_fusion
  59.1 1.5 multiply_convert_fusion
  60.6 1.5 fusion.3
  62.1 0.4 copy.52
  62.5 2.0 copy.51
  64.5 1.0 all_to_all.51
  65.5 0.7 copy.42
  66.2 4.0 %all-to-all-start.1 = ((bf16[4,128,256]{1,2,0:T(8,128)(2,1)}), bf16[4,128,256]{1,2,0:T(8,128)(2,1)}, u32[]{:S(2)}, u32[]{:S(2)}) async-start(bf16[4,128,256]{1,2,0:T(8,128)(2,1)} %copy.42), calls=%async_computation.1 | async-start | bytes 524288 | tf_op jit(solution)/shard_map/all_to_all | solution.py:134
  70.3 0.0 copy-start
  70.3 0.5 fusion.2
  70.7 0.4 copy.50
  71.2 4.5 %all-to-all-done.1 = bf16[4,128,256]{1,2,0:T(8,128)(2,1)} async-done(((bf16[4,128,256]{1,2,0:T(8,128)(2,1)}), bf16[4,128,256]{1,2,0:T(8,128)(2,1)}, u32[]{:S(2)}, u32[]{:S(2)}) %all-to-all-start.1) | async-done | bytes 262176 | tf_op jit(solution)/shard_map/all_to_all | solution.py:134
  75.7 1.1 copy.43
  76.8 0.1 broadcast_select_fusion
  76.9 3.4 %collective-permute-start = (bf16[15,1024]{1,0:T(8,128)(2,1)S(1)}, bf16[15,1024]{1,0:T(8,128)(2,1)S(1)}, u32[]{:S(2)}, u32[]{:S(2)}) collective-permute-start(bf16[15,1024]{1,0:T(8,128)(2,1)S(1)} %get-tuple-element.98), channel_id=1, source_target_pairs={{0,1},{1,2},{2,3},{4,5},{5,6},{6,7},{8,9},{9,10},{10,11},{12,13},{... | collective-permute-start | bytes 92168 | tf_op jit(solution)/shard_map/ppermute | solution.py:15
  80.3 3.8 %pad_maximum_fusion = bf16[3,512,256]{2,0,1:T(4,128)(2,1)} fusion(bf16[1,512,256]{2,0,1:T(2,128)(2,1)S(1)} %copy.52, bf16[1,512,256]{2,0,1:T(2,128)(2,1)} %copy.51, bf16[1,512,256]{2,0,1:T(2,128)(2,1)S(1)} %copy.50), kind=kLoop, calls=%fused_computation.101 | loop fusion | flops 2359296 | bytes 1572864 | tf_op jit(solution)/shard_map/stack | solution.py:163
  84.1 3.5 %all-to-all-start.3 = ((bf16[3,512,256]{2,0,1:T(4,128)(2,1)}), bf16[3,512,256]{2,0,1:T(4,128)(2,1)S(1)}, u32[]{:S(2)}, u32[]{:S(2)}) async-start(bf16[3,512,256]{2,0,1:T(4,128)(2,1)} %pad_maximum_fusion), calls=%async_computation.3 | async-start | bytes 2097152 | tf_op jit(solution)/shard_map/all_to_all | solution.py:170
  87.6 0.0 all-reduce.3.cloned.1.call-start
  87.7 1.3 collective-permute-start.1
  89.0 0.7 fusion.66
  89.7 0.5 fusion.65
  90.2 9.8 %collective-permute-done.1 = bf16[15,1024]{1,0:T(8,128)(2,1)S(1)} collective-permute-done((bf16[15,1024]{1,0:T(8,128)(2,1)S(1)}, bf16[15,1024]{1,0:T(8,128)(2,1)S(1)}, u32[]{:S(2)}, u32[]{:S(2)}) %collective-permute-start.1) | collective-permute-done | bytes 30752 | tf_op jit(solution)/shard_map/ppermute | solution.py:18
  100.0 0.5 fusion.81
  100.6 0.7 fusion.82
  101.2 2.7 %stack.135 = f32[31,1024]{1,0:T(8,128)} concatenate(f32[1,1024]{1,0:T(1,128)S(1)} %bitcast.220, f32[1,1024]{1,0:T(1,128)S(1)} %bitcast.221, f32[1,1024]{1,0:T(1,128)S(1)} %bitcast.222, f32[1,1024]{1,0:T(1,128)S(1)} %bitcast.223, f32[1,1024]{1,0:T(1,128)S(1)} %bitcast.224, f32[1,1024]{1,0:T(1,128)S(1)} %bitcast.225, f32[1,1024]{1,0:T(1,128)S(1)} %bitcast.226, ...), dimensions={0} | concatenate | bytes 253952 | tf_op jit(solution)/shard_map/stack | solution.py:109
  103.9 0.0 all-reduce.3.cloned.1.call-update
  103.9 0.0 all-reduce.5.cloned.1.call-start
  104.0 3.1 %fusion.139 = bf16[1,128,1024]{2,1,0:T(8,128)(2,1)} fusion(bf16[15,1024]{1,0:T(8,128)(2,1)S(1)} %collective-permute-done.1, bf16[128,1024]{1,0:T(8,128)(2,1)S(1)} %broadcast_select_fusion, f32[1024]{0:T(1024)S(1)} %bitcast.178, f32[1024]{0:T(1024)S(1)} %bitcast.180, f32[1024]{0:T(1024)S(1)} %bitcast.184, f32[1024]{0:T(1024)S(1)} %bitcast.186, ...), kind=kLoop, calls=%fused_computation.296 | loop fusion | flops 23986176 | bytes 712704 | tf_op jit(solution)/shard_map/broadcast_in_dim | solution.py:172
  107.1 39.4 %all-reduce.3.cloned.1.call-done = f32[31,1024]{1,0:T(8,128)} async-done(((f32[31,1024]{1,0:T(8,128)}), f32[31,1024]{1,0:T(8,128)}) %all-reduce.3.cloned.1.call-update) | async-done | bytes 126992 | tf_op jit(solution)/shard_map/psum | solution.py:146
  146.6 0.0 all-reduce.5.cloned.1.call-update
  146.6 1.1 fusion.140
  147.7 0.3 copy.55
  148.1 0.9 slice.517
  148.9 0.3 copy.54
  149.3 0.9 slice.515
  150.2 0.3 copy.53
  150.5 0.9 slice.513
  151.4 52.4 %all-reduce.5.cloned.1.call-done = f32[31,1024]{1,0:T(8,128)} async-done(((f32[31,1024]{1,0:T(8,128)}), f32[31,1024]{1,0:T(8,128)}) %all-reduce.5.cloned.1.call-update) | async-done | bytes 126992 | tf_op jit(solution)/shard_map/psum | solution.py:146
  203.8 1.6 copy.66
  (8 shorter events, 0.0 us)
Async XLA Ops:
  8.0 10.0 %collective-permute-start.2 = (bf16[15,1024]{1,0:T(8,128)(2,1)S(1)}, bf16[15,1024]{1,0:T(8,128)(2,1)S(1)}, u32[]{:S(2)}, u32[]{:S(2)}) collective-permute-start(bf16[15,1024]{1,0:T(8,128)(2,1)S(1)} %get-tuple-element.96), channel_id=1, source_target_pairs={{1,0},{2,1},{3,2},{5,4},{6,5},{7,6},{9,8},{10,9},{11,10},{13,12},{... | collective-permute-start | bytes 92168 | tf_op jit(solution)/shard_map/ppermute | solution.py:18
  9.3 8.7 %collective-permute-start.3 = (bf16[15,1024]{1,0:T(8,128)(2,1)S(1)}, bf16[15,1024]{1,0:T(8,128)(2,1)S(1)}, u32[]{:S(2)}, u32[]{:S(2)}) collective-permute-start(bf16[15,1024]{1,0:T(8,128)(2,1)S(1)} %get-tuple-element.97), channel_id=1, source_target_pairs={{0,1},{1,2},{2,3},{4,5},{5,6},{6,7},{8,9},{9,10},{10,11},{12,13},{... | collective-permute-start | bytes 92168 | tf_op jit(solution)/shard_map/ppermute | solution.py:15
  27.6 9.7 %all-to-all-start.2 = ((bf16[128,4,256]{0,2,1:T(8,128)(2,1)}), bf16[128,4,256]{0,2,1:T(8,128)(2,1)S(1)}, u32[]{:S(2)}, u32[]{:S(2)}) async-start(bf16[128,4,256]{0,2,1:T(8,128)(2,1)} %bitcast.41), calls=%async_computation.2 | async-start | bytes 524288 | tf_op jit(solution)/shard_map/all_to_all | solution.py:151
  37.3 15.8 %all-to-all-start = ((bf16[3,128,1024]{1,0,2:T(4,128)(2,1)}), bf16[3,128,1024]{1,0,2:T(4,128)(2,1)S(1)}, u32[]{:S(2)}, u32[]{:S(2)}) async-start(bf16[3,128,1024]{1,0,2:T(4,128)(2,1)} %copy.39), calls=%async_computation | async-start | bytes 2097152 | tf_op jit(solution)/shard_map/all_to_all | solution.py:127
  66.2 9.5 %all-to-all-start.1 = ((bf16[4,128,256]{1,2,0:T(8,128)(2,1)}), bf16[4,128,256]{1,2,0:T(8,128)(2,1)}, u32[]{:S(2)}, u32[]{:S(2)}) async-start(bf16[4,128,256]{1,2,0:T(8,128)(2,1)} %copy.42), calls=%async_computation.1 | async-start | bytes 524288 | tf_op jit(solution)/shard_map/all_to_all | solution.py:134
  70.3 18.7 %copy-start = (bf16[1,128,1024]{2,1,0:T(8,128)(2,1)S(1)}, bf16[1,128,1024]{2,1,0:T(8,128)(2,1)}, u32[]{:S(2)}) copy-start(bf16[1,128,1024]{2,1,0:T(8,128)(2,1)} %param.9) | copy-start | bytes 786436
  76.9 12.1 %collective-permute-start = (bf16[15,1024]{1,0:T(8,128)(2,1)S(1)}, bf16[15,1024]{1,0:T(8,128)(2,1)S(1)}, u32[]{:S(2)}, u32[]{:S(2)}) collective-permute-start(bf16[15,1024]{1,0:T(8,128)(2,1)S(1)} %get-tuple-element.98), channel_id=1, source_target_pairs={{0,1},{1,2},{2,3},{4,5},{5,6},{6,7},{8,9},{9,10},{10,11},{12,13},{... | collective-permute-start | bytes 92168 | tf_op jit(solution)/shard_map/ppermute | solution.py:15
  84.1 62.5 %all-to-all-start.3 = ((bf16[3,512,256]{2,0,1:T(4,128)(2,1)}), bf16[3,512,256]{2,0,1:T(4,128)(2,1)S(1)}, u32[]{:S(2)}, u32[]{:S(2)}) async-start(bf16[3,512,256]{2,0,1:T(4,128)(2,1)} %pad_maximum_fusion), calls=%async_computation.3 | async-start | bytes 2097152 | tf_op jit(solution)/shard_map/all_to_all | solution.py:170
  87.6 58.9 %all-reduce.3.cloned.1.call-start = ((), (), s32[]{:S(2)}) async-start(), calls=%async_computation.4 | async-start | bytes 262144 | tf_op jit(solution)/shard_map/psum | solution.py:146
  87.7 12.3 %collective-permute-start.1 = (bf16[15,1024]{1,0:T(8,128)(2,1)S(1)}, bf16[15,1024]{1,0:T(8,128)(2,1)S(1)}, u32[]{:S(2)}, u32[]{:S(2)}) collective-permute-start(bf16[15,1024]{1,0:T(8,128)(2,1)S(1)} %get-tuple-element.99), channel_id=1, source_target_pairs={{1,0},{2,1},{3,2},{5,4},{6,5},{7,6},{9,8},{10,9},{11,10},{13,12},{... | collective-permute-start | bytes 92168 | tf_op jit(solution)/shard_map/ppermute | solution.py:18
  103.9 99.9 %all-reduce.5.cloned.1.call-start = ((), (), s32[]{:S(2)}) async-start(), calls=%async_computation.5 | async-start | bytes 262144 | tf_op jit(solution)/shard_map/psum | solution.py:146
Sparse Core Ops, SparseCore 0:
  104.0 42.4 all-reduce.2
  148.9 54.8 all-reduce.4
